TPU v7x, 128 devices: a whole 4x4x4 slice. The times are simulated.
128 devices in a mesh: row: 16 (over z, x_hi, core), col: 8 (over x_lo, y).
Axes of the slice: x: 4 (x_hi: 2, x_lo: 2; x = x_hi * 2 + x_lo), y: 4, z: 4, core: 2. Of those that a mesh axis runs over, the one named last changes fastest.
Arguments:
- stored: bfloat16 [1024, 51200], P(('row', 'col')), may hold values from -24 to 24
- integrals: bfloat16 [51200, 25600], P('row', 'col'), may hold values from -0.02734375 to 0.02734375
- layout: int32 [1024], replicated, may hold values from 0 to 1023, each once
- partner: int32 [1024], replicated, may hold values from 0 to 1023, as said below
Outputs:
- residual_out: bfloat16 [1024, 25600], P('row', 'col')
Inputs may be any that keep to these rules, and one draw needn't show every extreme that they name: partner is an involution without fixed points: partner[p] != p and partner[partner[p]] = p. `layout`: each slab pair stands in exactly one stored row.
All inputs are finite; a program needn't handle non-finite values.
Results may differ from a plain program's by a relative error of at most 0.001.
Values may be sent and summed in bfloat16 or wider, within the bound.
A program may use at most 128 MiB of HBM per device.

v0:
```python
import jax
import jax.numpy as jnp
from jax import lax
from jax.sharding import Mesh, PartitionSpec as P

ROW_AXES = ("z", "xh", "core")
COL_AXES = ("xl", "y")


def per_device(stored, integrals, layout, partner):
    local_rows = stored.shape[0]
    n_z = lax.axis_size("z")
    n_xh = lax.axis_size("xh")
    n_core = lax.axis_size("core")
    n_row = n_z * n_xh * n_core
    n_col = lax.axis_size(COL_AXES)
    total = local_rows * n_row * n_col
    block = total // n_row
    regrouped = lax.all_to_all(stored, ROW_AXES, split_axis=1, concat_axis=0, tiled=True)
    gathered = lax.all_gather(regrouped, COL_AXES, axis=0, tiled=True)
    s = jnp.arange(total, dtype=jnp.int32)
    s_row = s // (local_rows * n_col)
    s_col = s // local_rows % n_col
    s_off = s % local_rows
    pos_of_stored = s_col * (n_row * local_rows) + s_row * local_rows + s_off
    inv = jnp.zeros((total,), jnp.int32).at[layout].set(s)
    i = jnp.arange(total, dtype=jnp.int32)
    g = i // block
    xh = g % n_xh
    core = g // n_xh % n_core
    z = g // (n_xh * n_core)
    p_of_i = ((z * n_xh + xh) * n_core + core) * block + i % block
    q = partner[p_of_i]
    q_g = q // block
    q_core = q_g % n_core
    q_xh = q_g // n_core % n_xh
    q_z = q_g // (n_core * n_xh)
    partner_i = ((q_z * n_core + q_core) * n_xh + q_xh) * block + q % block
    amps = gathered[pos_of_stored[inv[p_of_i]]]
    ladder = jnp.dot(amps, integrals, preferred_element_type=jnp.float32)
    difference = ladder - ladder[partner_i]
    part = lax.psum_scatter(difference, ("z", "core"), scatter_dimension=0, tiled=True)
    part = lax.psum_scatter(part, "xh", scatter_dimension=0, tiled=True)
    return part.astype(jnp.bfloat16)


def solution(mesh):
    n_row, n_col = mesh.devices.shape
    fine = Mesh(mesh.devices.reshape(4, n_row // 8, 2, 2, n_col // 2), ROW_AXES + COL_AXES)
    return jax.shard_map(
        per_device,
        mesh=fine,
        in_specs=(P(ROW_AXES + COL_AXES, None), P(ROW_AXES, COL_AXES), P(), P()),
        out_specs=P(ROW_AXES, COL_AXES),
        check_vma=False,
    )
```

profile of v0, /device:TPU:1, one launch (start us, length us, event | category | flops | bytes accessed | tf_op | source)
XLA Modules:
  0.0 296.2 jit_solution(10515165706835330987)
XLA Ops:
  6.5 0.0 copy-start
  6.5 0.0 all-gather.2.cloned.1.call-start
  6.5 24.0 %all_to_all.19 = bf16[8,16,3200]{2,0,1:T(8,128)(2,1)} all-to-all(bf16[8,16,3200]{2,0,1:T(8,128)(2,1)} %bitcast.15), channel_id=1, replica_groups=mesh['z'=4,'xh'=2,'core'=2,'xl'=2,'y'=4] {'z','xh','core'}, dimensions={1} | all-to-all | bytes 1638400 | tf_op jit(solution)/shard_map/all_to_all | solution.py:19
  30.6 0.0 all-gather.2.cloned.1.call-update
  30.6 0.0 reduce-scatter.3.cloned.1.call-start
  30.7 0.0 copy-done
  30.7 4.5 %gather_fusion.3 = s32[1024]{0:T(1024)S(1)} fusion(s32[1024]{0:T(1024)S(1)} %copy-done, s32[1024]{0:T(1024)S(1)} %broadcast_clamp_fusion.1), kind=kCustom, calls=%fused_computation.3 | custom fusion | bytes 12288 | tf_op jit(solution)/shard_map/gather | solution.py:33
  35.2 0.7 compare_select_fusion.8
  35.9 4.3 %scatter_custom_fusion = s32[1024]{0:T(1024)S(1)} fusion(s32[1024]{0:T(1024)S(1)} %compare_select_fusion.8, s32[1024]{0:T(1024)S(1)} %iota.13, s32[]{:T(128)} %constant.129.clone.1), kind=kCustom, calls=%fused_computation.79 | custom fusion | bytes 4100 | tf_op jit(solution)/shard_map/scatter | solution.py:26
  40.3 4.5 %gather_fusion = s32[1024]{0:T(1024)S(1)} fusion(s32[1024]{0:T(1024)S(1)} %scatter_custom_fusion, s32[1024]{0:T(1024)S(1)} %broadcast_clamp_fusion.1), kind=kCustom, calls=%fused_computation | custom fusion | bytes 12288 | tf_op jit(solution)/shard_map/gather | solution.py:39
  44.8 4.5 %gather_fusion.1 = s32[1024]{0:T(1024)S(1)} fusion(s32[1024]{0:T(1024)S(1)} %get-tuple-element.5, s32[1024]{0:T(1024)S(1)} %get-tuple-element.6), kind=kCustom, calls=%fused_computation.1 | custom fusion | bytes 12288 | tf_op jit(solution)/shard_map/gather | solution.py:39
  49.4 0.1 compare_select_fusion
  49.5 53.2 %all-gather.2.cloned.1.call-done = bf16[1024,3200]{1,0:T(8,128)(2,1)} async-done(((bf16[128,3200]{1,0:T(8,128)(2,1)}), bf16[1024,3200]{1,0:T(8,128)(2,1)}) %all-gather.2.cloned.1.call-update) | async-done | bytes 6553616 | tf_op jit(solution)/shard_map/all_gather | solution.py:20
  102.7 16.3 %gather_fusion.2 = bf16[1024,3200]{1,0:T(8,128)(2,1)} fusion(bf16[1024,3200]{1,0:T(8,128)(2,1)} %all-gather.2.cloned.1.call-done, s32[1024]{0:T(1024)S(1)} %broadcast_clamp_fusion.3), kind=kCustom, calls=%fused_computation.2 | custom fusion | bytes 13111296 | tf_op jit(solution)/shard_map/gather | solution.py:39
  119.0 30.5 %fusion.24 = f32[1024,3200]{1,0:T(8,128)} fusion(bf16[1024,3200]{1,0:T(8,128)(2,1)} %gather_fusion.2, bf16[3200,3200]{1,0:T(8,128)(2,1)} %param.5), kind=kOutput, calls=%fused_computation.81 | convolution fusion | flops 20971520000 | bytes 40140800 | tf_op jit(solution)/shard_map/dot_general | solution.py:40
  149.5 17.1 %gather_fusion.4 = f32[1024,3200]{1,0:T(8,128)} fusion(f32[1024,3200]{1,0:T(8,128)} %fusion.24, s32[1024]{0:T(1024)S(1)} %broadcast_clamp_fusion), kind=kCustom, calls=%fused_computation.4 | custom fusion | bytes 26218496 | tf_op jit(solution)/shard_map/gather | solution.py:41
  166.7 0.0 copy-start.1
  166.7 14.4 %sub.51 = f32[1024,3200]{1,0:T(8,128)} subtract(f32[1024,3200]{1,0:T(8,128)} %fusion.24, f32[1024,3200]{1,0:T(8,128)} %gather_fusion.4) | non-fusion elementwise | flops 3276800 | bytes 39321600 | tf_op jit(solution)/shard_map/sub | solution.py:41
  181.0 0.0 reduce-scatter.3.cloned.1.call-update
  181.1 0.0 reduce-scatter.5.cloned.1.call-start
  181.1 73.3 %reduce-scatter.3.cloned.1.call-done = f32[128,3200]{1,0:T(8,128)} async-done(((f32[1024,3200]{1,0:T(8,128)}), f32[128,3200]{1,0:T(8,128)}) %reduce-scatter.3.cloned.1.call-update) | async-done | bytes 1638416 | tf_op jit(solution)/shard_map/reduce_scatter | solution.py:42
  254.4 0.0 reduce-scatter.5.cloned.1.call-update
  254.4 33.4 %reduce-scatter.5.cloned.1.call-done = f32[64,3200]{1,0:T(8,128)} async-done(((f32[128,3200]{1,0:T(8,128)}), f32[64,3200]{1,0:T(8,128)}) %reduce-scatter.5.cloned.1.call-update) | async-done | bytes 819216 | tf_op jit(solution)/shard_map/reduce_scatter | solution.py:43
  287.8 1.9 convert_element_type.3
  289.7 0.0 copy-done.1
  (8 shorter events, 0.1 us)
Async XLA Ops:
  6.5 24.2 %copy-start = (s32[1024]{0:T(1024)S(1)}, s32[1024]{0:T(1024)}, u32[]{:S(2)}) copy-start(s32[1024]{0:T(1024)} %param.7) | copy-start | bytes 12292
  6.5 96.2 %all-gather.2.cloned.1.call-start = ((), (), s32[]{:S(2)}) async-start(), calls=%async_computation.3 | async-start | bytes 7372800 | tf_op jit(solution)/shard_map/all_gather | solution.py:20
  30.6 223.8 %reduce-scatter.3.cloned.1.call-start = ((), (), s32[]{:S(2)}) async-start(), calls=%async_computation.4 | async-start | bytes 14745600 | tf_op jit(solution)/shard_map/reduce_scatter | solution.py:42
  166.7 123.1 %copy-start.1 = (s32[1024]{0:T(1024)S(1)}, s32[1024]{0:T(1024)}, u32[]{:S(2)}) copy-start(s32[1024]{0:T(1024)} %param.7) | copy-start | bytes 12292
  181.1 106.7 %reduce-scatter.5.cloned.1.call-start = ((), (), s32[]{:S(2)}) async-start(), calls=%async_computation.5 | async-start | bytes 2457600 | tf_op jit(solution)/shard_map/reduce_scatter | solution.py:43
Sparse Core Ops, SparseCore 0:
  30.7 71.9 all-gather.1
  181.2 73.1 reduce-scatter.2
  256.7 30.9 reduce-scatter.4
where the time goes:
time: 297 us; the launch traced here: 296 us
  waiting for transfers between devices  160 us (54%)
  local copies, waits for them, and re-layouts  51.3 us (17%)
  matrix products  30.5 us (10%)
  blocking collectives  24 us (8%)
  other arithmetic  17.2 us (6%)
  between operations  13.2 us (4%)
    reduce_scatter x1, waiting for transfers between devices, per_device(): lax.psum_scatter(difference, ('z', 'core'), scatter_dimension=0, tiled=True)  73.3 us
    all_gather x1, waiting for transfers between devices, per_device(): gathered = lax.all_gather(regrouped, COL_AXES, axis=0, tiled=True)  53.2 us
    reduce_scatter x1, waiting for transfers between devices, per_device(): part = lax.psum_scatter(part, 'xh', scatter_dimension=0, tiled=True)  33.4 us
    dot_general x1, matrix products, per_device(): ladder = jnp.dot(amps, integrals, preferred_element_type=jnp.float32)  30.5 us
    gather x3, local copies, waits for them, and re-layouts, per_device(): amps = gathered[pos_of_stored[inv[p_of_i]]]  25.3 us
    all_to_all x1, blocking collectives, per_device(): lax.all_to_all(stored, ROW_AXES, split_axis=1, concat_axis=0, tiled=True)  24 us
    gather x1, local copies, waits for them, and re-layouts, per_device(): difference = ladder - ladder[partner_i]  17.1 us
    sub x1, other arithmetic, per_device(): difference = ladder - ladder[partner_i]  14.4 us
  transfers between devices with their start and end apart: 3, of which 3 were waited for; matrix products, arithmetic and copies ran while one was open for 6% of the time, Pallas kernels for 0%

commit v1 on v0

--- a/solution.py
+++ b/solution.py
@@ -17,7 +17,9 @@
     total = local_rows * n_row * n_col
     block = total // n_row
     regrouped = lax.all_to_all(stored, ROW_AXES, split_axis=1, concat_axis=0, tiled=True)
-    gathered = lax.all_gather(regrouped, COL_AXES, axis=0, tiled=True)
+    gathered = jnp.concatenate(
+        lax.all_to_all(jnp.stack([regrouped] * lax.axis_size(COL_AXES)), COL_AXES, 0, 0), axis=0
+    )
     s = jnp.arange(total, dtype=jnp.int32)
     s_row = s // (local_rows * n_col)
     s_col = s // local_rows % n_col

time: 297 us -> 305 us (1.027)
  starting transfers between devices: 0.09 us -> 4.86 us
  local copies, waits for them, and re-layouts: 51.3 us -> 54.9 us
    all_to_all x0 -> x1, waiting for transfers between devices: none -> 55.9 us  [per_device(): lax.all_to_all(jnp.stack([regrouped] * lax.axis_size(COL_AXES)), COL_AXES...]
    all_gather x1 -> x0, waiting for transfers between devices: 53.2 us -> none  [per_device(): gathered = lax.all_gather(regrouped, COL_AXES, axis=0, tiled=True)]
    all_to_all x0 -> x1, starting transfers between devices: none -> 4.78 us  [per_device(): lax.all_to_all(jnp.stack([regrouped] * lax.axis_size(COL_AXES)), COL_AXES...]
    another operation x0 -> x1, local copies, waits for them, and re-layouts: none -> 3.52 us  [per_device(): jnp.stack([regrouped] * lax.axis_size(COL_AXES))]
where the time goes in v1:
time: 305 us
  waiting for transfers between devices  160 us (52%)
  local copies, waits for them, and re-layouts  54.9 us (18%)
  matrix products  30.5 us (10%)
  blocking collectives  23.9 us (8%)
  other arithmetic  16.5 us (5%)
  between operations  13.5 us (4%)
  starting transfers between devices  4.86 us (2%)
    reduce_scatter x1, waiting for transfers between devices, per_device(): lax.psum_scatter(difference, ('z', 'core'), scatter_dimension=0, tiled=True)  71.1 us
    all_to_all x1, waiting for transfers between devices, per_device(): lax.all_to_all(jnp.stack([regrouped] * lax.axis_size(COL_AXES)), COL_AXES...  55.9 us
    reduce_scatter x1, waiting for transfers between devices, per_device(): part = lax.psum_scatter(part, 'xh', scatter_dimension=0, tiled=True)  33.3 us
    dot_general x1, matrix products, per_device(): ladder = jnp.dot(amps, integrals, preferred_element_type=jnp.float32)  30.5 us
    gather x3, local copies, waits for them, and re-layouts, per_device(): amps = gathered[pos_of_stored[inv[p_of_i]]]  25.3 us
    all_to_all x1, blocking collectives, per_device(): lax.all_to_all(stored, ROW_AXES, split_axis=1, concat_axis=0, tiled=True)  23.9 us
    gather x1, local copies, waits for them, and re-layouts, per_device(): difference = ladder - ladder[partner_i]  17.1 us
    sub x1, other arithmetic, per_device(): difference = ladder - ladder[partner_i]  14.4 us
  transfers between devices with their start and end apart: 3, of which 3 were waited for; matrix products, arithmetic and copies ran while one was open for 6% of the time, Pallas kernels for 0%

profile of v1, /device:TPU:1, one launch (start us, length us, event | category | flops | bytes accessed | tf_op | source)
XLA Modules:
  0.0 304.5 jit_solution(3793737830031540644)
XLA Ops:
  6.5 0.0 copy-start
  6.5 0.0 copy-start.2
  6.5 23.9 %all_to_all.21 = bf16[8,16,3200]{2,0,1:T(8,128)(2,1)S(1)} all-to-all(bf16[8,16,3200]{2,0,1:T(8,128)(2,1)} %bitcast.16), channel_id=1, replica_groups=mesh['z'=4,'xh'=2,'core'=2,'xl'=2,'y'=4] {'z','xh','core'}, dimensions={1} | all-to-all | bytes 1638400 | tf_op jit(solution)/shard_map/all_to_all | solution.py:19
  30.5 3.5 %stack.5 = bf16[8,128,3200]{2,1,0:T(8,128)(2,1)} broadcast(bf16[128,3200]{1,0:T(8,128)(2,1)S(1)} %bitcast.15), dimensions={1,2} | broadcast | bytes 7372800 | tf_op jit(solution)/shard_map/stack | solution.py:21
  34.0 4.8 %all-to-all-start.1 = ((bf16[8,128,3200]{2,1,0:T(8,128)(2,1)}), bf16[8,128,3200]{2,1,0:T(8,128)(2,1)}, u32[]{:S(2)}, u32[]{:S(2)}) async-start(bf16[8,128,3200]{2,1,0:T(8,128)(2,1)} %stack.5), calls=%async_computation.1 | async-start | bytes 13107200 | tf_op jit(solution)/shard_map/all_to_all | solution.py:21
  38.8 0.0 reduce-scatter.3.cloned.1.call-start
  38.9 0.0 copy-done
  38.9 4.5 %gather_fusion.3 = s32[1024]{0:T(1024)S(1)} fusion(s32[1024]{0:T(1024)S(1)} %copy-done, s32[1024]{0:T(1024)S(1)} %broadcast_clamp_fusion.1), kind=kCustom, calls=%fused_computation.3 | custom fusion | bytes 12288 | tf_op jit(solution)/shard_map/gather | solution.py:35
  43.4 0.0 copy-done.2
  43.5 4.3 %scatter_custom_fusion = s32[1024]{0:T(1024)S(1)} fusion(s32[1024]{0:T(1024)S(1)} %compare_select_fusion.8, s32[1024]{0:T(1024)S(1)} %iota.13, s32[]{:T(128)} %constant.129.clone.1), kind=kCustom, calls=%fused_computation.79 | custom fusion | bytes 4100 | tf_op jit(solution)/shard_map/scatter | solution.py:28
  47.8 4.5 %gather_fusion = s32[1024]{0:T(1024)S(1)} fusion(s32[1024]{0:T(1024)S(1)} %scatter_custom_fusion, s32[1024]{0:T(1024)S(1)} %broadcast_clamp_fusion.1), kind=kCustom, calls=%fused_computation | custom fusion | bytes 12288 | tf_op jit(solution)/shard_map/gather | solution.py:41
  52.3 4.5 %gather_fusion.1 = s32[1024]{0:T(1024)S(1)} fusion(s32[1024]{0:T(1024)S(1)} %get-tuple-element.5, s32[1024]{0:T(1024)S(1)} %get-tuple-element.6), kind=kCustom, calls=%fused_computation.1 | custom fusion | bytes 12288 | tf_op jit(solution)/shard_map/gather | solution.py:41
  56.9 0.1 compare_select_fusion
  57.0 55.9 %all-to-all-done.1 = bf16[8,128,3200]{2,1,0:T(8,128)(2,1)} async-done(((bf16[8,128,3200]{2,1,0:T(8,128)(2,1)}), bf16[8,128,3200]{2,1,0:T(8,128)(2,1)}, u32[]{:S(2)}, u32[]{:S(2)}) %all-to-all-start.1) | async-done | bytes 6553632 | tf_op jit(solution)/shard_map/all_to_all | solution.py:21
  112.9 16.3 %gather_fusion.2 = bf16[1024,3200]{1,0:T(8,128)(2,1)} fusion(bf16[1024,3200]{1,0:T(8,128)(2,1)} %bitcast.3, s32[1024]{0:T(1024)S(1)} %broadcast_clamp_fusion.3), kind=kCustom, calls=%fused_computation.2 | custom fusion | bytes 13111296 | tf_op jit(solution)/shard_map/gather | solution.py:41
  129.2 30.5 %fusion.24 = f32[1024,3200]{1,0:T(8,128)} fusion(bf16[1024,3200]{1,0:T(8,128)(2,1)} %gather_fusion.2, bf16[3200,3200]{1,0:T(8,128)(2,1)} %param.5), kind=kOutput, calls=%fused_computation.81 | convolution fusion | flops 20971520000 | bytes 40140800 | tf_op jit(solution)/shard_map/dot_general | solution.py:42
  159.7 17.1 %gather_fusion.4 = f32[1024,3200]{1,0:T(8,128)} fusion(f32[1024,3200]{1,0:T(8,128)} %fusion.24, s32[1024]{0:T(1024)S(1)} %broadcast_clamp_fusion), kind=kCustom, calls=%fused_computation.4 | custom fusion | bytes 26218496 | tf_op jit(solution)/shard_map/gather | solution.py:43
  176.8 0.0 copy-start.1
  176.9 14.4 %sub.51 = f32[1024,3200]{1,0:T(8,128)} subtract(f32[1024,3200]{1,0:T(8,128)} %fusion.24, f32[1024,3200]{1,0:T(8,128)} %gather_fusion.4) | non-fusion elementwise | flops 3276800 | bytes 39321600 | tf_op jit(solution)/shard_map/sub | solution.py:43
  191.2 0.0 reduce-scatter.3.cloned.1.call-update
  191.3 0.0 reduce-scatter.5.cloned.1.call-start
  191.3 71.1 %reduce-scatter.3.cloned.1.call-done = f32[128,3200]{1,0:T(8,128)} async-done(((f32[1024,3200]{1,0:T(8,128)}), f32[128,3200]{1,0:T(8,128)}) %reduce-scatter.3.cloned.1.call-update) | async-done | bytes 1638416 | tf_op jit(solution)/shard_map/reduce_scatter | solution.py:44
  262.4 0.0 reduce-scatter.5.cloned.1.call-update
  262.4 33.3 %reduce-scatter.5.cloned.1.call-done = f32[64,3200]{1,0:T(8,128)} async-done(((f32[128,3200]{1,0:T(8,128)}), f32[64,3200]{1,0:T(8,128)}) %reduce-scatter.5.cloned.1.call-update) | async-done | bytes 819216 | tf_op jit(solution)/shard_map/reduce_scatter | solution.py:45
  295.8 1.9 convert_element_type.3
  297.7 0.0 copy-done.1
  (9 shorter events, 0.1 us)
Async XLA Ops:
  6.5 32.4 %copy-start = (s32[1024]{0:T(1024)S(1)}, s32[1024]{0:T(1024)}, u32[]{:S(2)}) copy-start(s32[1024]{0:T(1024)} %param.7) | copy-start | bytes 12292
  6.5 36.9 %copy-start.2 = (s32[1024]{0:T(1024)S(1)}, s32[1024]{0:T(1024)}, u32[]{:S(2)}) copy-start(s32[1024]{0:T(1024)} %param.6) | copy-start | bytes 12292
  34.0 78.9 %all-to-all-start.1 = ((bf16[8,128,3200]{2,1,0:T(8,128)(2,1)}), bf16[8,128,3200]{2,1,0:T(8,128)(2,1)}, u32[]{:S(2)}, u32[]{:S(2)}) async-start(bf16[8,128,3200]{2,1,0:T(8,128)(2,1)} %stack.5), calls=%async_computation.1 | async-start | bytes 13107200 | tf_op jit(solution)/shard_map/all_to_all | solution.py:21
  38.8 223.6 %reduce-scatter.3.cloned.1.call-start = ((), (), s32[]{:S(2)}) async-start(), calls=%async_computation.4 | async-start | bytes 14745600 | tf_op jit(solution)/shard_map/reduce_scatter | solution.py:44
  176.8 120.8 %copy-start.1 = (s32[1024]{0:T(1024)S(1)}, s32[1024]{0:T(1024)}, u32[]{:S(2)}) copy-start(s32[1024]{0:T(1024)} %param.7) | copy-start | bytes 12292
  191.3 104.5 %reduce-scatter.5.cloned.1.call-start = ((), (), s32[]{:S(2)}) async-start(), calls=%async_computation.5 | async-start | bytes 2457600 | tf_op jit(solution)/shard_map/reduce_scatter | solution.py:45
Sparse Core Ops, SparseCore 0:
  191.4 70.9 reduce-scatter.2
  264.7 30.9 reduce-scatter.4
